TPU v7x, 256 devices: a whole 4x4x8 slice. The times are simulated.
256 devices in a mesh: dp: 32 (over z, x), pipe: 2 (over core), tensor: 4 (over y).
Axes of the slice: x: 4, y: 4, z: 8, core: 2. Of those that a mesh axis runs over, the one named last changes fastest.
Arguments:
- tokens: bfloat16 [64, 64, 4096], P('dp', None, 'tensor'), may hold values from -8 to 8
- w_query: bfloat16 [2, 2, 4096, 4096], P(None, 'pipe', 'dp', 'tensor'), may hold values from -8 to 8
- w_key: bfloat16 [2, 2, 4096, 1024], P(None, 'pipe', 'dp', 'tensor'), may hold values from -1 to 1
- w_value: bfloat16 [2, 2, 4096, 1024], P(None, 'pipe', 'dp', 'tensor'), may hold values from -0.09375 to 0.09375
- w_out: bfloat16 [2, 2, 4096, 4096], P(None, 'pipe', 'tensor', 'dp'), may hold values from -0.09375 to 0.09375
- norm_gain: float32 [2, 2, 4096], P(None, 'pipe'), may hold values from 0.5 to 1.5
- boundary: int32 [64], P('dp'), may hold values from 1 to 63
- skip_offset: int32 [64], P('dp'), may hold values from 0 to 131008
- doc_lengths: int32 [64, 4], P('dp'), may hold values from 1 to 32, 64 in all within a row
- batch_order: int32 [32, 2], P('dp'), may hold values from 0 to 1, each once within a row
Outputs:
- final_state: bfloat16 [64, 64, 4096], P('dp', 'pipe', 'tensor')
Inputs may be any that keep to these rules, and one draw needn't show every extreme that they name: `doc_lengths`: each row sums to 64. `batch_order`: each row is a permutation.
All inputs are finite; a program needn't handle non-finite values.
Results may differ from a plain program's by a relative error of at most 0.014.
Values may be sent and summed in bfloat16 or wider, within the bound.
A program may use at most 192 MiB of HBM per device.

v0:
```python
from functools import partial
import jax
import jax.numpy as jnp
from jax import lax
from jax.sharding import PartitionSpec as P

HEAD_DIM = 128
ROPE_THETA = 500000.0
NORM_EPSILON = 1e-05


def cut_along(value, dim, peers):
    before, after = (value.shape[:dim], value.shape[dim + 1 :])
    return jnp.moveaxis(value.reshape(*before, peers, -1, *after), dim, 0)


def sent_and_summed(value, axis, dim):
    peers = lax.axis_size(axis)
    blocks = lax.all_to_all(cut_along(value, dim, peers), axis, 0, 0, tiled=True)
    return jnp.sum(blocks, axis=0)


def sent_together(arrays, axis, dim, along):
    widths = [a.shape[along] for a in arrays]
    both = jnp.concatenate(arrays, axis=along)
    whole = lax.all_gather(both, axis, axis=dim, tiled=True)
    return tuple(jnp.split(whole, [sum(widths[:k]) for k in range(1, len(widths))], axis=along))


def from_behind(value, axis, by):
    peers = lax.axis_size(axis)
    pairs = [(i, i + by) for i in range(peers) if 0 <= i + by < peers]
    return lax.ppermute(value, axis, pairs)


def picked(value, axis, root):
    return lax.dynamic_index_in_dim(lax.all_gather(value, axis), root, 0, keepdims=False)


def rope_angles(positions, head_dim):
    half_dim = head_dim // 2
    exponent = jnp.arange(half_dim, dtype=jnp.float32) * (2.0 / head_dim)
    frequency = jnp.float32(ROPE_THETA) ** (-exponent)
    return positions.astype(jnp.float32)[..., None] * frequency


def rotate(values, angles):
    half_dim = values.shape[-1] // 2
    first_half = values[..., :half_dim]
    second = values[..., half_dim:]
    cosine = jnp.cos(angles)[:, None, :]
    sine_part = jnp.sin(angles)[:, None, :]
    return jnp.concatenate(
        [first_half * cosine - second * sine_part, second * cosine + first_half * sine_part],
        axis=-1,
    )


def sample_layout(first_cut, offset, lengths, seq_len):
    places = jnp.arange(seq_len, dtype=jnp.int32)
    positions = jnp.where(places < first_cut, places, places + offset)
    doc_ends = jnp.cumsum(lengths)
    doc_ids = jnp.sum((places[:, None] >= doc_ends[None, :]).astype(jnp.int32), axis=1)
    allowed = (doc_ids[:, None] == doc_ids[None, :]) & (places[None, :] <= places[:, None])
    return (positions, allowed)


def attend(normed, q_weight, k_weight, v_weight, angles, allowed):
    seq_len = normed.shape[0]
    q_heads = q_weight.shape[1] // HEAD_DIM
    kv_heads = k_weight.shape[1] // HEAD_DIM
    group_size = q_heads // kv_heads
    queries = jnp.dot(normed, q_weight, preferred_element_type=jnp.float32)
    key_vecs = jnp.dot(normed, k_weight, preferred_element_type=jnp.float32)
    value_vecs = jnp.dot(normed, v_weight, preferred_element_type=jnp.float32).astype(jnp.bfloat16)
    value_vecs = value_vecs.reshape(seq_len, kv_heads, HEAD_DIM)
    queries = rotate(queries.reshape(seq_len, q_heads, HEAD_DIM), angles).astype(jnp.bfloat16)
    queries = queries.reshape(seq_len, kv_heads, group_size, HEAD_DIM)
    key_vecs = rotate(key_vecs.reshape(seq_len, kv_heads, HEAD_DIM), angles).astype(jnp.bfloat16)
    scores = jnp.einsum(
        "skgd,tkd->kgst", queries, key_vecs, preferred_element_type=jnp.float32
    ) * HEAD_DIM ** (-0.5)
    scores = jnp.where(allowed[None, None], scores, -jnp.inf)
    row_max = jnp.max(scores, axis=-1, keepdims=True)
    exp_scores = jnp.exp(scores - row_max)
    weights = (exp_scores / jnp.sum(exp_scores, axis=-1, keepdims=True)).astype(jnp.bfloat16)
    mixed = jnp.einsum("kgst,tkd->skgd", weights, value_vecs, preferred_element_type=jnp.float32)
    return mixed.reshape(seq_len, q_heads * HEAD_DIM)


def layer_step(stream, active, gain_row, weight_three, out_part, angles, allowed):
    gathered = lax.all_gather(stream, "tensor", axis=1, tiled=True)
    seq_len = gathered.shape[0]
    head_width = weight_three[0].shape[1]

    def local_mix():
        widened = gathered.astype(jnp.float32)
        inv_rms = lax.rsqrt(jnp.mean(widened * widened, axis=-1, keepdims=True) + NORM_EPSILON)
        normed = (widened * inv_rms * gain_row).astype(jnp.bfloat16)
        return attend(
            normed, weight_three[0], weight_three[1], weight_three[2], angles, allowed
        ).astype(jnp.bfloat16)

    mixed = lax.cond(active, local_mix, lambda: jnp.zeros((seq_len, head_width), jnp.bfloat16))
    partial_sum = lax.cond(
        active,
        lambda: jnp.dot(mixed, out_part, preferred_element_type=jnp.float32),
        lambda: jnp.zeros((mixed.shape[0], out_part.shape[1]), jnp.float32),
    )
    shares = sent_and_summed(partial_sum, "tensor", 1)
    updated = (stream.astype(jnp.float32) + shares).astype(jnp.bfloat16)
    return jnp.where(active, updated, jnp.zeros_like(updated))


def per_device(
    tokens,
    w_query,
    w_key,
    w_value,
    w_out,
    norm_gain,
    boundary,
    skip_offset,
    doc_lengths,
    batch_order,
):
    sections = lax.axis_size("pipe")
    my_section = lax.axis_index("pipe")
    micro_count = tokens.shape[0]
    seq_len = tokens.shape[1]
    local_width = tokens.shape[2]
    ordered = batch_order[0]
    doc_costs = jnp.sum(doc_lengths * doc_lengths, axis=1)
    slot_cost = jnp.take(doc_costs, ordered)
    slot_of = jnp.argsort(-slot_cost, stable=True)
    samples = jnp.take(ordered, slot_of)
    feed_rows = jnp.take(tokens, samples, axis=0)
    positions, allowed = jax.vmap(partial(sample_layout, seq_len=seq_len))(
        jnp.take(boundary, samples),
        jnp.take(skip_offset, samples),
        jnp.take(doc_lengths, samples, axis=0),
    )
    angles = rope_angles(positions, HEAD_DIM)
    down_gain = norm_gain[0, 0]
    up_gain = norm_gain[1, 0]
    out_full = lax.all_gather(w_out, "dp", axis=3, tiled=True)
    down_out_part = out_full[0, 0]
    up_out_part = out_full[1, 0]
    query_full, key_full, value_full = sent_together((w_query, w_key, w_value), "dp", 2, 3)
    down_three = (query_full[0, 0], key_full[0, 0], value_full[0, 0])
    up_three = (query_full[1, 0], key_full[1, 0], value_full[1, 0])
    step_count = micro_count + 2 * sections - 2
    empty_rows = jnp.zeros((seq_len, local_width), jnp.bfloat16)
    last_item = micro_count - 1

    def select_item(stacked, item_index):
        return lax.dynamic_index_in_dim(
            stacked, jnp.clip(item_index, 0, last_item), 0, keepdims=False
        )

    def advance(tick_now, loop_state):
        down_buf, up_buf, results, up_weights = loop_state
        down_item = tick_now - my_section
        down_ok = (down_item >= 0) & (down_item < micro_count)
        down_in = jnp.where(my_section == 0, select_item(feed_rows, tick_now), down_buf)
        down_out = layer_step(
            down_in,
            down_ok,
            down_gain,
            down_three,
            down_out_part,
            select_item(angles, down_item),
            select_item(allowed, down_item),
        )
        up_item = tick_now - (2 * sections - 2 - my_section)
        up_ok = (up_item >= 0) & (up_item < micro_count)
        up_in = jnp.where(my_section == sections - 1, down_out, up_buf)
        up_out = layer_step(
            up_in,
            up_ok,
            up_gain,
            up_weights,
            up_out_part,
            select_item(angles, up_item),
            select_item(allowed, up_item),
        )
        out_slot = select_item(slot_of, up_item)
        stored = lax.dynamic_update_index_in_dim(results, up_out, out_slot, 0)
        results = jnp.where(up_ok & (my_section == 0), stored, results)
        down_buf = from_behind(down_out, "pipe", 1)
        up_buf = from_behind(up_out, "pipe", -1)
        return (down_buf, up_buf, results, up_weights)

    initial = (
        empty_rows,
        empty_rows,
        jnp.zeros((micro_count, seq_len, local_width), jnp.bfloat16),
        up_three,
    )
    down_buf, up_buf, results, up_weights = lax.fori_loop(0, step_count, advance, initial)
    spread = picked(results, "pipe", 0)
    row_count = seq_len // sections
    return lax.dynamic_slice_in_dim(spread, my_section * row_count, row_count, 1)


def solution(mesh):
    placed = (
        P("dp", None, "tensor"),
        P(None, "pipe", "dp", "tensor"),
        P(None, "pipe", "dp", "tensor"),
        P(None, "pipe", "dp", "tensor"),
        P(None, "pipe", "tensor", "dp"),
        P(None, "pipe", None),
        P("dp"),
        P("dp"),
        P("dp", None),
        P("dp", None),
    )
    return jax.shard_map(
        per_device, mesh=mesh, in_specs=placed, out_specs=P("dp", "pipe", "tensor"), check_vma=False
    )
```

profile of v0, /device:TPU:1, one launch (start us, length us, event | category | flops | bytes accessed | tf_op | source)
XLA Modules:
  0.0 725.0 jit_solution(7644802526432635606)
XLA Ops:
  7.3 2.1 pad_maximum_fusion
  22.8 136.4 %all-gather.6.cloned.1.call-done = bf16[2,1,1024,4096]{3,2,1,0:T(8,128)(2,1)} async-done(((bf16[2,1,1024,128]{3,2,1,0:T(8,128)(2,1)}), bf16[2,1,1024,4096]{3,2,1,0:T(8,128)(2,1)}) %all-gather.6.cloned.1.call-update) | async-done | bytes 16777232 | tf_op jit(solution)/shard_map/all_gather | solution.py:146
  159.2 11.7 %slice_bitcast_fusion = (bf16[1024,4096]{1,0:T(8,128)(2,1)}, bf16[1024,4096]{1,0:T(8,128)(2,1)}) fusion(bf16[2,1,1024,4096]{3,2,1,0:T(8,128)(2,1)} %all-gather.6.cloned.1.call-done), kind=kLoop, calls=%fused_computation.98 | loop fusion | bytes 33554432 | tf_op jit(solution)/shard_map/squeeze | solution.py:148
  170.9 174.1 %all-gather.4.cloned.1.call-done = bf16[2,1,4096,1536]{3,2,1,0:T(8,128)(2,1)} async-done(((bf16[2,1,128,1536]{3,2,1,0:T(8,128)(2,1)}), bf16[2,1,4096,1536]{3,2,1,0:T(8,128)(2,1)}) %all-gather.4.cloned.1.call-update) | async-done | bytes 25165840 | tf_op jit(solution)/shard_map/all_gather | solution.py:26
  345.0 6.3 slice_bitcast_fusion.4
  351.3 11.6 %slice_bitcast_fusion.1 = (bf16[4096,1024]{1,0:T(8,128)(2,1)}, bf16[4096,1024]{1,0:T(8,128)(2,1)}) fusion(bf16[2,1,4096,1536]{3,2,1,0:T(8,128)(2,1)} %all-gather.4.cloned.1.call-done), kind=kLoop, calls=%fused_computation.99 | loop fusion | bytes 33554432 | tf_op jit(solution)/shard_map/squeeze | solution.py:151
  363.6 351.6 %while.19 = (s32[]{:T(128)}, bf16[64,1024]{1,0:T(8,128)(2,1)}, bf16[64,1024]{1,0:T(8,128)(2,1)S(1)}, bf16[2,64,1024]{2,1,0:T(8,128)(2,1)S(1)}, s32[]{:T(128)}, /...) while((s32[]{:T(128)}, bf16[64,1024]{1,0:T(8,128)(2,1)}, ...), condition=%wide.region_21.23_spmd.clone, body=%wide.region_4.22_spmd.clone.sunk | while | flops 2746410496 | bytes 85502200 | solution.py:200
  364.6 11.5 %all_gather.36 = bf16[64,4096]{1,0:T(8,128)(2,1)S(1)} all-gather(bf16[64,1024]{1,0:T(8,128)(2,1)S(1)} %bitcast_select_fusion.3), channel_id=1, replica_groups=mesh['dp'=32,'pipe'=2,'tensor'=4] {'tensor'}, dimensions={1}, use_global_device_ids=true | all-gather | bytes 655360 | tf_op jit(solution)/shard_map/while/body/eval_jaxpr/all_gather | solution.py:92
  378.5 1.6 copy.113
  380.1 3.5 all-to-all-start
  383.7 9.7 %all-to-all-done = f32[4,64,1024]{2,1,0:T(8,128)S(1)} async-done(((f32[4,64,1024]{2,1,0:T(8,128)}), f32[4,64,1024]{2,1,0:T(8,128)S(1)}, u32[]{:S(2)}, u32[]{:S(2)}) %all-to-all-start) | async-done | bytes 1048608 | tf_op jit(solution)/shard_map/while/body/eval_jaxpr/all_to_all | solution.py:19
  394.2 9.9 %all_gather.37 = bf16[64,4096]{1,0:T(8,128)(2,1)S(1)} all-gather(bf16[64,1024]{1,0:T(8,128)(2,1)S(1)} %get-tuple-element.869), channel_id=1, replica_groups=mesh['dp'=32,'pipe'=2,'tensor'=4] {'tensor'}, dimensions={1}, use_global_device_ids=true | all-gather | bytes 655360 | tf_op jit(solution)/shard_map/while/body/eval_jaxpr/all_gather | solution.py:92
  404.9 1.6 copy.114
  406.5 3.5 all-to-all-start.1
  413.6 6.4 all-to-all-done.1
  420.2 26.8 %collective-permute-start.1 = (bf16[64,1024]{1,0:T(8,128)(2,1)S(1)}, bf16[64,1024]{1,0:T(8,128)(2,1)S(1)}, u32[]{:S(2)}, u32[]{:S(2)}) collective-permute-start(bf16[64,1024]{1,0:T(8,128)(2,1)S(1)} %get-tuple-element.870), channel_id=1, source_target_pairs={{4,0},{5,1},{6,2},{7,3},{12,8},{13,9},{14,10},{15,11},{20,16},{21,... | collective-permute-start | bytes 393224 | tf_op jit(solution)/shard_map/while/body/eval_jaxpr/ppermute | solution.py:33
  448.9 9.9 %all_gather.36 = bf16[64,4096]{1,0:T(8,128)(2,1)S(1)} all-gather(bf16[64,1024]{1,0:T(8,128)(2,1)S(1)} %bitcast_select_fusion.3), channel_id=1, replica_groups=mesh['dp'=32,'pipe'=2,'tensor'=4] {'tensor'}, dimensions={1}, use_global_device_ids=true | all-gather | bytes 655360 | tf_op jit(solution)/shard_map/while/body/eval_jaxpr/all_gather | solution.py:92
  460.4 11.3 %conditional.12 = (bf16[64,1024]{1,0:T(8,128)(2,1)S(1)}) conditional(s32[]{:T(128)} %convert_element_type.206, () %tuple.107, (bf16[64,4096]{1,0:T(8,128)(2,1)S(1)}, f32[1,1,4096]{2,1,0:T(1,128)S(1)}, bf16[4096,256]{1,0:T(8,128)(2,1)}, s32[]{:T(128)}, pred[2,64,64]{1,2,0:T(8,128)(4,1)S(1)}, /*index=5*/bf16[4096,256]{1,0:T(8,128)(2,1)}, ...), branch_computations={%region_5.6_spmd, %region_6.10_spmd} | conditional | flops 835764928 | bytes 17847848 | solution.py:104
  460.7 2.1 fusion.41
  463.2 5.0 convolution_bitcast_fusion
  468.8 2.1 convolution_convert_fusion.1
  471.7 5.0 conditional.13
  471.8 4.9 fusion.100
  477.4 1.6 copy.113
  479.0 3.5 all-to-all-start
  482.6 11.3 %all-to-all-done = f32[4,64,1024]{2,1,0:T(8,128)S(1)} async-done(((f32[4,64,1024]{2,1,0:T(8,128)}), f32[4,64,1024]{2,1,0:T(8,128)S(1)}, u32[]{:S(2)}, u32[]{:S(2)}) %all-to-all-start) | async-done | bytes 1048608 | tf_op jit(solution)/shard_map/while/body/eval_jaxpr/all_to_all | solution.py:19
  494.7 10.7 %all_gather.37 = bf16[64,4096]{1,0:T(8,128)(2,1)S(1)} all-gather(bf16[64,1024]{1,0:T(8,128)(2,1)S(1)} %get-tuple-element.869), channel_id=1, replica_groups=mesh['dp'=32,'pipe'=2,'tensor'=4] {'tensor'}, dimensions={1}, use_global_device_ids=true | all-gather | bytes 655360 | tf_op jit(solution)/shard_map/while/body/eval_jaxpr/all_gather | solution.py:92
  505.4 11.5 %conditional.14 = (bf16[64,1024]{1,0:T(8,128)(2,1)S(1)}) conditional(s32[]{:T(128)} %convert_element_type.207, () %tuple.111, (bf16[64,4096]{1,0:T(8,128)(2,1)S(1)}, f32[1,1,4096]{2,1,0:T(1,128)S(1)}, bf16[4096,256]{1,0:T(8,128)(2,1)}, pred[2,64,64]{1,2,0:T(8,128)(4,1)S(1)}, s32[]{:T(128)}, /*index=5*/bf16[4096,256]{1,0:T(8,128)(2,1)}, ...), branch_computations={%region_13.14_spmd, %region_14.18_spmd} | conditional | flops 835764928 | bytes 26319488 | solution.py:104
  505.6 2.1 fusion.81
  508.1 5.2 convolution_bitcast_fusion.1
  516.9 5.0 conditional.15
  517.0 5.0 fusion.101
  522.7 1.6 copy.114
  524.3 3.5 all-to-all-start.1
  531.4 6.1 all-to-all-done.1
  540.9 9.9 %all_gather.36 = bf16[64,4096]{1,0:T(8,128)(2,1)S(1)} all-gather(bf16[64,1024]{1,0:T(8,128)(2,1)S(1)} %bitcast_select_fusion.3), channel_id=1, replica_groups=mesh['dp'=32,'pipe'=2,'tensor'=4] {'tensor'}, dimensions={1}, use_global_device_ids=true | all-gather | bytes 655360 | tf_op jit(solution)/shard_map/while/body/eval_jaxpr/all_gather | solution.py:92
  552.4 11.3 %conditional.12 = (bf16[64,1024]{1,0:T(8,128)(2,1)S(1)}) conditional(s32[]{:T(128)} %convert_element_type.206, () %tuple.107, (bf16[64,4096]{1,0:T(8,128)(2,1)S(1)}, f32[1,1,4096]{2,1,0:T(1,128)S(1)}, bf16[4096,256]{1,0:T(8,128)(2,1)}, s32[]{:T(128)}, pred[2,64,64]{1,2,0:T(8,128)(4,1)S(1)}, /*index=5*/bf16[4096,256]{1,0:T(8,128)(2,1)}, ...), branch_computations={%region_5.6_spmd, %region_6.10_spmd} | conditional | flops 835764928 | bytes 17847848 | solution.py:104
  552.6 2.1 fusion.41
  555.1 5.0 convolution_bitcast_fusion
  560.8 2.1 convolution_convert_fusion.1
  563.7 5.0 conditional.13
  563.7 4.9 fusion.100
  569.4 1.6 copy.113
  571.0 3.5 all-to-all-start
  574.5 10.6 %all-to-all-done = f32[4,64,1024]{2,1,0:T(8,128)S(1)} async-done(((f32[4,64,1024]{2,1,0:T(8,128)}), f32[4,64,1024]{2,1,0:T(8,128)S(1)}, u32[]{:S(2)}, u32[]{:S(2)}) %all-to-all-start) | async-done | bytes 1048608 | tf_op jit(solution)/shard_map/while/body/eval_jaxpr/all_to_all | solution.py:19
  586.0 9.9 %all_gather.37 = bf16[64,4096]{1,0:T(8,128)(2,1)S(1)} all-gather(bf16[64,1024]{1,0:T(8,128)(2,1)S(1)} %get-tuple-element.869), channel_id=1, replica_groups=mesh['dp'=32,'pipe'=2,'tensor'=4] {'tensor'}, dimensions={1}, use_global_device_ids=true | all-gather | bytes 655360 | tf_op jit(solution)/shard_map/while/body/eval_jaxpr/all_gather | solution.py:92
  595.8 11.5 %conditional.14 = (bf16[64,1024]{1,0:T(8,128)(2,1)S(1)}) conditional(s32[]{:T(128)} %convert_element_type.207, () %tuple.111, (bf16[64,4096]{1,0:T(8,128)(2,1)S(1)}, f32[1,1,4096]{2,1,0:T(1,128)S(1)}, bf16[4096,256]{1,0:T(8,128)(2,1)}, pred[2,64,64]{1,2,0:T(8,128)(4,1)S(1)}, s32[]{:T(128)}, /*index=5*/bf16[4096,256]{1,0:T(8,128)(2,1)}, ...), branch_computations={%region_13.14_spmd, %region_14.18_spmd} | conditional | flops 835764928 | bytes 26319488 | solution.py:104
  596.1 2.1 fusion.81
  598.6 5.1 convolution_bitcast_fusion.1
  607.4 5.0 conditional.15
  607.4 5.0 fusion.101
  613.1 1.6 copy.114
  614.7 3.5 all-to-all-start.1
  621.8 6.1 all-to-all-done.1
  631.4 9.9 %all_gather.36 = bf16[64,4096]{1,0:T(8,128)(2,1)S(1)} all-gather(bf16[64,1024]{1,0:T(8,128)(2,1)S(1)} %bitcast_select_fusion.3), channel_id=1, replica_groups=mesh['dp'=32,'pipe'=2,'tensor'=4] {'tensor'}, dimensions={1}, use_global_device_ids=true | all-gather | bytes 655360 | tf_op jit(solution)/shard_map/while/body/eval_jaxpr/all_gather | solution.py:92
  643.7 1.6 copy.113
  645.3 3.5 all-to-all-start
  648.8 11.3 %all-to-all-done = f32[4,64,1024]{2,1,0:T(8,128)S(1)} async-done(((f32[4,64,1024]{2,1,0:T(8,128)}), f32[4,64,1024]{2,1,0:T(8,128)S(1)}, u32[]{:S(2)}, u32[]{:S(2)}) %all-to-all-start) | async-done | bytes 1048608 | tf_op jit(solution)/shard_map/while/body/eval_jaxpr/all_to_all | solution.py:19
  661.0 10.7 %all_gather.37 = bf16[64,4096]{1,0:T(8,128)(2,1)S(1)} all-gather(bf16[64,1024]{1,0:T(8,128)(2,1)S(1)} %get-tuple-element.869), channel_id=1, replica_groups=mesh['dp'=32,'pipe'=2,'tensor'=4] {'tensor'}, dimensions={1}, use_global_device_ids=true | all-gather | bytes 655360 | tf_op jit(solution)/shard_map/while/body/eval_jaxpr/all_gather | solution.py:92
  672.5 1.6 copy.114
  674.1 3.5 all-to-all-start.1
  681.2 6.1 all-to-all-done.1
  687.5 26.7 %collective-permute-start.1 = (bf16[64,1024]{1,0:T(8,128)(2,1)S(1)}, bf16[64,1024]{1,0:T(8,128)(2,1)S(1)}, u32[]{:S(2)}, u32[]{:S(2)}) collective-permute-start(bf16[64,1024]{1,0:T(8,128)(2,1)S(1)} %get-tuple-element.870), channel_id=1, source_target_pairs={{4,0},{5,1},{6,2},{7,3},{12,8},{13,9},{14,10},{15,11},{20,16},{21,... | collective-permute-start | bytes 393224 | tf_op jit(solution)/shard_map/while/body/eval_jaxpr/ppermute | solution.py:33
  715.2 2.3 all-gather
  (208 shorter events, 61.9 us)
Async XLA Ops:
  6.5 11.5 %copy-start = (bf16[2,64,1024]{2,1,0:T(8,128)(2,1)S(1)}, bf16[2,64,1024]{2,1,0:T(8,128)(2,1)}, u32[]{:S(2)}) copy-start(bf16[2,64,1024]{2,1,0:T(8,128)(2,1)} %param.22) | copy-start | bytes 786436
  6.5 152.7 %all-gather.6.cloned.1.call-start = ((), (), s32[]{:S(2)}) async-start(), calls=%async_computation.3 | async-start | bytes 17301504 | tf_op jit(solution)/shard_map/all_gather | solution.py:146
  7.3 337.8 %all-gather.4.cloned.1.call-start = ((), (), s32[]{:S(2)}) async-start(), calls=%async_computation.2 | async-start | bytes 25952256 | tf_op jit(solution)/shard_map/all_gather | solution.py:26
  12.8 3.9 copy-start.7
  380.1 13.2 %all-to-all-start = ((f32[4,64,1024]{2,1,0:T(8,128)}), f32[4,64,1024]{2,1,0:T(8,128)S(1)}, u32[]{:S(2)}, u32[]{:S(2)}) async-start(f32[4,64,1024]{2,1,0:T(8,128)} %copy.113), calls=%async_computation | async-start | bytes 2097152 | tf_op jit(solution)/shard_map/while/body/eval_jaxpr/all_to_all | solution.py:19
  404.1 6.0 copy-start.8
  404.1 8.2 %copy-start.3 = (bf16[64,1024]{1,0:T(8,128)(2,1)S(1)}, bf16[64,1024]{1,0:T(8,128)(2,1)}, u32[]{:S(2)}) copy-start(bf16[64,1024]{1,0:T(8,128)(2,1)} %get-tuple-element.868) | copy-start | bytes 393220 | tf_op jit(solution)/shard_map/while
  406.5 13.5 %all-to-all-start.1 = ((f32[4,64,1024]{2,1,0:T(8,128)}), f32[4,64,1024]{2,1,0:T(8,128)S(1)}, u32[]{:S(2)}, u32[]{:S(2)}) async-start(f32[4,64,1024]{2,1,0:T(8,128)} %copy.114), calls=%async_computation.1 | async-start | bytes 2097152 | tf_op jit(solution)/shard_map/while/body/eval_jaxpr/all_to_all | solution.py:19
  412.3 34.6 %collective-permute-start = (bf16[64,1024]{1,0:T(8,128)(2,1)S(1)}, bf16[64,1024]{1,0:T(8,128)(2,1)}, u32[]{:S(2)}, u32[]{:S(2)}) collective-permute-start(bf16[64,1024]{1,0:T(8,128)(2,1)S(1)} %copy-done.3), channel_id=1, source_target_pairs={{0,4},{1,5},{2,6},{3,7},{8,12},{9,13},{10,14},{11,15},{16,20},{17,... | collective-permute-start | bytes 393224 | tf_op jit(solution)/shard_map/while/body/eval_jaxpr/ppermute | solution.py:33
  420.2 27.7 %collective-permute-start.1 = (bf16[64,1024]{1,0:T(8,128)(2,1)S(1)}, bf16[64,1024]{1,0:T(8,128)(2,1)S(1)}, u32[]{:S(2)}, u32[]{:S(2)}) collective-permute-start(bf16[64,1024]{1,0:T(8,128)(2,1)S(1)} %get-tuple-element.870), channel_id=1, source_target_pairs={{4,0},{5,1},{6,2},{7,3},{12,8},{13,9},{14,10},{15,11},{20,16},{21,... | collective-permute-start | bytes 393224 | tf_op jit(solution)/shard_map/while/body/eval_jaxpr/ppermute | solution.py:33
  479.0 14.9 %all-to-all-start = ((f32[4,64,1024]{2,1,0:T(8,128)}), f32[4,64,1024]{2,1,0:T(8,128)S(1)}, u32[]{:S(2)}, u32[]{:S(2)}) async-start(f32[4,64,1024]{2,1,0:T(8,128)} %copy.113), calls=%async_computation | async-start | bytes 2097152 | tf_op jit(solution)/shard_map/while/body/eval_jaxpr/all_to_all | solution.py:19
  505.6 2.5 copy-start.5
  508.1 5.5 copy-start.4
  508.1 6.1 copy-start.2
  513.6 0.6 copy-start.6
  516.9 10.9 %copy-start.8 = (s32[2]{0:T(128)S(1)}, s32[2]{0:T(128)}, u32[]{:S(2)}) copy-start(s32[2]{0:T(128)} %get-tuple-element.947) | copy-start | bytes 28 | tf_op jit(solution)/shard_map/while
  516.9 13.2 %copy-start.3 = (bf16[64,1024]{1,0:T(8,128)(2,1)S(1)}, bf16[64,1024]{1,0:T(8,128)(2,1)}, u32[]{:S(2)}) copy-start(bf16[64,1024]{1,0:T(8,128)(2,1)} %get-tuple-element.868) | copy-start | bytes 393220 | tf_op jit(solution)/shard_map/while
  524.3 13.2 %all-to-all-start.1 = ((f32[4,64,1024]{2,1,0:T(8,128)}), f32[4,64,1024]{2,1,0:T(8,128)S(1)}, u32[]{:S(2)}, u32[]{:S(2)}) async-start(f32[4,64,1024]{2,1,0:T(8,128)} %copy.114), calls=%async_computation.1 | async-start | bytes 2097152 | tf_op jit(solution)/shard_map/while/body/eval_jaxpr/all_to_all | solution.py:19
  530.1 8.9 %collective-permute-start = (bf16[64,1024]{1,0:T(8,128)(2,1)S(1)}, bf16[64,1024]{1,0:T(8,128)(2,1)}, u32[]{:S(2)}, u32[]{:S(2)}) collective-permute-start(bf16[64,1024]{1,0:T(8,128)(2,1)S(1)} %copy-done.3), channel_id=1, source_target_pairs={{0,4},{1,5},{2,6},{3,7},{8,12},{9,13},{10,14},{11,15},{16,20},{17,... | collective-permute-start | bytes 393224 | tf_op jit(solution)/shard_map/while/body/eval_jaxpr/ppermute | solution.py:33
  537.6 2.3 collective-permute-start.1
  571.0 14.2 %all-to-all-start = ((f32[4,64,1024]{2,1,0:T(8,128)}), f32[4,64,1024]{2,1,0:T(8,128)S(1)}, u32[]{:S(2)}, u32[]{:S(2)}) async-start(f32[4,64,1024]{2,1,0:T(8,128)} %copy.113), calls=%async_computation | async-start | bytes 2097152 | tf_op jit(solution)/shard_map/while/body/eval_jaxpr/all_to_all | solution.py:19
  596.1 2.5 copy-start.5
  598.5 5.5 copy-start.4
  598.6 6.1 copy-start.2
  604.0 0.6 copy-start.6
  607.4 10.9 %copy-start.8 = (s32[2]{0:T(128)S(1)}, s32[2]{0:T(128)}, u32[]{:S(2)}) copy-start(s32[2]{0:T(128)} %get-tuple-element.947) | copy-start | bytes 28 | tf_op jit(solution)/shard_map/while
  607.4 13.2 %copy-start.3 = (bf16[64,1024]{1,0:T(8,128)(2,1)S(1)}, bf16[64,1024]{1,0:T(8,128)(2,1)}, u32[]{:S(2)}) copy-start(bf16[64,1024]{1,0:T(8,128)(2,1)} %get-tuple-element.868) | copy-start | bytes 393220 | tf_op jit(solution)/shard_map/while
  614.7 13.2 %all-to-all-start.1 = ((f32[4,64,1024]{2,1,0:T(8,128)}), f32[4,64,1024]{2,1,0:T(8,128)S(1)}, u32[]{:S(2)}, u32[]{:S(2)}) async-start(f32[4,64,1024]{2,1,0:T(8,128)} %copy.114), calls=%async_computation.1 | async-start | bytes 2097152 | tf_op jit(solution)/shard_map/while/body/eval_jaxpr/all_to_all | solution.py:19
  620.5 8.9 %collective-permute-start = (bf16[64,1024]{1,0:T(8,128)(2,1)S(1)}, bf16[64,1024]{1,0:T(8,128)(2,1)}, u32[]{:S(2)}, u32[]{:S(2)}) collective-permute-start(bf16[64,1024]{1,0:T(8,128)(2,1)S(1)} %copy-done.3), channel_id=1, source_target_pairs={{0,4},{1,5},{2,6},{3,7},{8,12},{9,13},{10,14},{11,15},{16,20},{17,... | collective-permute-start | bytes 393224 | tf_op jit(solution)/shard_map/while/body/eval_jaxpr/ppermute | solution.py:33
  628.1 2.3 collective-permute-start.1
  645.3 14.9 %all-to-all-start = ((f32[4,64,1024]{2,1,0:T(8,128)}), f32[4,64,1024]{2,1,0:T(8,128)S(1)}, u32[]{:S(2)}, u32[]{:S(2)}) async-start(f32[4,64,1024]{2,1,0:T(8,128)} %copy.113), calls=%async_computation | async-start | bytes 2097152 | tf_op jit(solution)/shard_map/while/body/eval_jaxpr/all_to_all | solution.py:19
  671.7 6.0 copy-start.8
  671.7 8.2 %copy-start.3 = (bf16[64,1024]{1,0:T(8,128)(2,1)S(1)}, bf16[64,1024]{1,0:T(8,128)(2,1)}, u32[]{:S(2)}) copy-start(bf16[64,1024]{1,0:T(8,128)(2,1)} %get-tuple-element.868) | copy-start | bytes 393220 | tf_op jit(solution)/shard_map/while
  674.1 13.2 %all-to-all-start.1 = ((f32[4,64,1024]{2,1,0:T(8,128)}), f32[4,64,1024]{2,1,0:T(8,128)S(1)}, u32[]{:S(2)}, u32[]{:S(2)}) async-start(f32[4,64,1024]{2,1,0:T(8,128)} %copy.114), calls=%async_computation.1 | async-start | bytes 2097152 | tf_op jit(solution)/shard_map/while/body/eval_jaxpr/all_to_all | solution.py:19
  679.9 34.3 %collective-permute-start = (bf16[64,1024]{1,0:T(8,128)(2,1)S(1)}, bf16[64,1024]{1,0:T(8,128)(2,1)}, u32[]{:S(2)}, u32[]{:S(2)}) collective-permute-start(bf16[64,1024]{1,0:T(8,128)(2,1)S(1)} %copy-done.3), channel_id=1, source_target_pairs={{0,4},{1,5},{2,6},{3,7},{8,12},{9,13},{10,14},{11,15},{16,20},{17,... | collective-permute-start | bytes 393224 | tf_op jit(solution)/shard_map/while/body/eval_jaxpr/ppermute | solution.py:33
  687.5 27.7 %collective-permute-start.1 = (bf16[64,1024]{1,0:T(8,128)(2,1)S(1)}, bf16[64,1024]{1,0:T(8,128)(2,1)S(1)}, u32[]{:S(2)}, u32[]{:S(2)}) collective-permute-start(bf16[64,1024]{1,0:T(8,128)(2,1)S(1)} %get-tuple-element.870), channel_id=1, source_target_pairs={{4,0},{5,1},{6,2},{7,3},{12,8},{13,9},{14,10},{15,11},{20,16},{21,... | collective-permute-start | bytes 393224 | tf_op jit(solution)/shard_map/while/body/eval_jaxpr/ppermute | solution.py:33
  715.2 3.0 copy-start.1
Sparse Core Ops, SparseCore 0:
  9.8 149.3 all-gather.5
  161.8 183.1 all-gather.3
where the time goes:
time: 727 us; the launch traced here: 725 us
  waiting for transfers between devices  383 us (53%)
  starting transfers between devices  89.4 us (12%)
  blocking collectives  84.6 us (12%)
  local copies, waits for them, and re-layouts  62.1 us (9%)
  matrix products  60.5 us (8%)
  other arithmetic  24 us (3%)
  between operations  13.5 us (2%)
  loops' own time  8.27 us (1%)
    all_gather x1, waiting for transfers between devices, sent_together(): whole = lax.all_gather(both, axis, axis=dim, tiled=True)  174 us
    all_gather x1, waiting for transfers between devices, per_device(): out_full = lax.all_gather(w_out, 'dp', axis=3, tiled=True)  136 us
    all_gather x8, blocking collectives, layer_step(): gathered = lax.all_gather(stream, 'tensor', axis=1, tiled=True)  82.3 us
    all_to_all x8, waiting for transfers between devices, sent_and_summed(): lax.all_to_all(cut_along(value, dim, peers), axis, 0, 0, tiled=True)  67.7 us
    ppermute x8, starting transfers between devices, from_behind(): return lax.ppermute(value, axis, pairs)  61.2 us
    all_to_all x8, starting transfers between devices, sent_and_summed(): lax.all_to_all(cut_along(value, dim, peers), axis, 0, 0, tiled=True)  28.1 us
    dot_general x4, matrix products, attend(): queries = jnp.dot(normed, q_weight, preferred_element_type=jnp.float32)  20.3 us
    dot_general x4, matrix products, layer_step(): jnp.dot(mixed, out_part, preferred_element_type=jnp.float32)  19.8 us
  transfers between devices with their start and end apart: 18, of which 14 were waited for; matrix products, arithmetic and copies ran while one was open for 4% of the time, Pallas kernels for 0%

commit v1 on v0

--- a/solution.py
+++ b/solution.py
@@ -143,7 +143,9 @@
     angles = rope_angles(positions, HEAD_DIM)
     down_gain = norm_gain[0, 0]
     up_gain = norm_gain[1, 0]
-    out_full = lax.all_gather(w_out, "dp", axis=3, tiled=True)
+    out_full = jnp.concatenate(
+        lax.all_to_all(jnp.stack([w_out] * lax.axis_size("dp")), "dp", 0, 0), axis=3
+    )
     down_out_part = out_full[0, 0]
     up_out_part = out_full[1, 0]
     query_full, key_full, value_full = sent_together((w_query, w_key, w_value), "dp", 2, 3)

time: 727 us -> 991 us (1.36)
  the two profiles are of different devices: /device:TPU:1 before, /device:TPU:199 now
where the time goes in v1:
time: 991 us; the launch traced here: 988 us
  waiting for transfers between devices  591 us (60%)
  local copies, waits for them, and re-layouts  111 us (11%)
  starting transfers between devices  98.3 us (10%)
  blocking collectives  83 us (8%)
  matrix products  60.4 us (6%)
  other arithmetic  22.1 us (2%)
  between operations  13.5 us (1%)
    all_to_all x1, waiting for transfers between devices, per_device(): lax.all_to_all(jnp.stack([w_out] * lax.axis_size('dp')), 'dp', 0, 0)  520 us
    all_gather x8, blocking collectives, layer_step(): gathered = lax.all_gather(stream, 'tensor', axis=1, tiled=True)  80.7 us
    all_to_all x8, waiting for transfers between devices, sent_and_summed(): lax.all_to_all(cut_along(value, dim, peers), axis, 0, 0, tiled=True)  66.5 us
    ppermute x8, starting transfers between devices, from_behind(): return lax.ppermute(value, axis, pairs)  61.7 us
    all_to_all x8, starting transfers between devices, sent_and_summed(): lax.all_to_all(cut_along(value, dim, peers), axis, 0, 0, tiled=True)  28.1 us
    unnamed x18, local copies, waits for them, and re-layouts  23.5 us
    all_to_all x1, local copies, waits for them, and re-layouts, per_device(): lax.all_to_all(jnp.stack([w_out] * lax.axis_size('dp')), 'dp', 0, 0)  21.2 us
    dot_general x4, matrix products, attend(): queries = jnp.dot(normed, q_weight, preferred_element_type=jnp.float32)  20.3 us
  transfers between devices with their start and end apart: 18, of which 13 were waited for; matrix products, arithmetic and copies ran while one was open for 8% of the time, Pallas kernels for 0%

profile of v1, /device:TPU:199, one launch (start us, length us, event | category | flops | bytes accessed | tf_op | source)
XLA Modules:
  0.0 988.0 jit_solution(6784506779217757122)
XLA Ops:
  6.5 2.1 pad_maximum_fusion
  8.7 7.0 stack.2
  15.7 8.5 all-to-all-start.2
  32.4 520.5 %all-to-all-done.2 = bf16[32,2,1,1024,128]{4,3,2,1,0:T(8,128)(2,1)} async-done(((bf16[32,2,1,1024,128]{4,3,2,1,0:T(8,128)(2,1)}), bf16[32,2,1,1024,128]{4,3,2,1,0:T(8,128)(2,1)}, u32[]{:S(2)}, u32[]{:S(2)}) %all-to-all-start.2) | async-done | bytes 16777248 | tf_op jit(solution)/shard_map/all_to_all | solution.py:147
  552.8 21.2 %copy.86 = bf16[32,2,1,1024,128]{3,4,0,2,1:T(8,128)(2,1)} copy(bf16[32,2,1,1024,128]{4,3,2,1,0:T(8,128)(2,1)} %all-to-all-done.2) | data formatting | bytes 33554432 | tf_op jit(solution)/shard_map/all_to_all | solution.py:147
  574.0 11.9 %fusion.99 = (bf16[1,1,1024,32,128]{2,4,3,1,0:T(8,128)(2,1)}, bf16[1,1,1024,32,128]{2,4,3,1,0:T(8,128)(2,1)}) fusion(bf16[2,1,1024,32,128]{2,4,3,1,0:T(8,128)(2,1)} %bitcast.140), kind=kLoop, calls=%fused_computation.131 | loop fusion | bytes 33554432 | tf_op jit(solution)/shard_map/slice | solution.py:150
  585.9 12.0 %copy.87 = bf16[1024,4096]{1,0:T(8,128)(2,1)} copy(bf16[1024,4096]{0,1:T(8,128)(2,1)} %bitcast.144) | data formatting | bytes 16777216
  597.9 11.4 %copy.88 = bf16[1024,4096]{1,0:T(8,128)(2,1)} copy(bf16[1024,4096]{0,1:T(8,128)(2,1)} %bitcast.143) | data formatting | bytes 16777216
  609.4 6.3 slice_bitcast_fusion.2
  615.7 11.6 %slice_bitcast_fusion = (bf16[4096,1024]{1,0:T(8,128)(2,1)}, bf16[4096,1024]{1,0:T(8,128)(2,1)}) fusion(bf16[2,1,4096,1536]{3,2,1,0:T(8,128)(2,1)} %all-gather.3.cloned.1.call-done), kind=kLoop, calls=%fused_computation.98 | loop fusion | bytes 33554432 | tf_op jit(solution)/shard_map/squeeze | solution.py:153
  628.0 350.2 %while.19 = (s32[]{:T(128)}, bf16[64,1024]{1,0:T(8,128)(2,1)}, bf16[64,1024]{1,0:T(8,128)(2,1)S(1)}, bf16[2,64,1024]{2,1,0:T(8,128)(2,1)S(1)}, s32[]{:T(128)}, /...) while((s32[]{:T(128)}, bf16[64,1024]{1,0:T(8,128)(2,1)}, ...), condition=%wide.region_21.23_spmd.clone, body=%wide.region_4.22_spmd.clone.sunk | while | flops 2746410496 | bytes 85502200 | solution.py:202
  629.2 9.9 %all_gather.32 = bf16[64,4096]{1,0:T(8,128)(2,1)S(1)} all-gather(bf16[64,1024]{1,0:T(8,128)(2,1)S(1)} %bitcast_select_fusion.3), channel_id=1, replica_groups=mesh['dp'=32,'pipe'=2,'tensor'=4] {'tensor'}, dimensions={1}, use_global_device_ids=true | all-gather | bytes 655360 | tf_op jit(solution)/shard_map/while/body/eval_jaxpr/all_gather | solution.py:92
  641.6 1.6 copy.119
  643.2 3.5 all-to-all-start
  646.7 9.7 all-to-all-done
  657.2 9.9 %all_gather.33 = bf16[64,4096]{1,0:T(8,128)(2,1)S(1)} all-gather(bf16[64,1024]{1,0:T(8,128)(2,1)S(1)} %get-tuple-element.917), channel_id=1, replica_groups=mesh['dp'=32,'pipe'=2,'tensor'=4] {'tensor'}, dimensions={1}, use_global_device_ids=true | all-gather | bytes 655360 | tf_op jit(solution)/shard_map/while/body/eval_jaxpr/all_gather | solution.py:92
  668.0 1.6 copy.120
  669.5 3.5 all-to-all-start.1
  676.9 5.9 all-to-all-done.1
  682.9 27.2 %collective-permute-start.1 = (bf16[64,1024]{1,0:T(8,128)(2,1)S(1)}, bf16[64,1024]{1,0:T(8,128)(2,1)S(1)}, u32[]{:S(2)}, u32[]{:S(2)}) collective-permute-start(bf16[64,1024]{1,0:T(8,128)(2,1)S(1)} %get-tuple-element.918), channel_id=1, source_target_pairs={{4,0},{5,1},{6,2},{7,3},{12,8},{13,9},{14,10},{15,11},{20,16},{21,... | collective-permute-start | bytes 393224 | tf_op jit(solution)/shard_map/while/body/eval_jaxpr/ppermute | solution.py:33
  712.1 9.9 %all_gather.32 = bf16[64,4096]{1,0:T(8,128)(2,1)S(1)} all-gather(bf16[64,1024]{1,0:T(8,128)(2,1)S(1)} %bitcast_select_fusion.3), channel_id=1, replica_groups=mesh['dp'=32,'pipe'=2,'tensor'=4] {'tensor'}, dimensions={1}, use_global_device_ids=true | all-gather | bytes 655360 | tf_op jit(solution)/shard_map/while/body/eval_jaxpr/all_gather | solution.py:92
  723.7 11.3 %conditional.12 = (bf16[64,1024]{1,0:T(8,128)(2,1)S(1)}) conditional(s32[]{:T(128)} %convert_element_type.206, () %tuple.109, (bf16[64,4096]{1,0:T(8,128)(2,1)S(1)}, f32[1,1,4096]{2,1,0:T(1,128)S(1)}, bf16[4096,256]{1,0:T(8,128)(2,1)}, s32[]{:T(128)}, pred[2,64,64]{1,2,0:T(8,128)(4,1)S(1)}, /*index=5*/bf16[4096,256]{1,0:T(8,128)(2,1)}, ...), branch_computations={%region_5.6_spmd, %region_6.10_spmd} | conditional | flops 835764928 | bytes 17847848 | solution.py:104
  723.9 2.1 fusion.41
  726.4 5.0 convolution_bitcast_fusion
  732.1 2.1 convolution_convert_fusion.1
  735.0 5.0 conditional.13
  735.0 4.9 fusion.101
  740.7 1.6 copy.119
  742.2 3.5 all-to-all-start
  745.8 11.3 %all-to-all-done = f32[4,64,1024]{2,1,0:T(8,128)S(1)} async-done(((f32[4,64,1024]{2,1,0:T(8,128)}), f32[4,64,1024]{2,1,0:T(8,128)S(1)}, u32[]{:S(2)}, u32[]{:S(2)}) %all-to-all-start) | async-done | bytes 1048608 | tf_op jit(solution)/shard_map/while/body/eval_jaxpr/all_to_all | solution.py:19
  757.9 10.7 %all_gather.33 = bf16[64,4096]{1,0:T(8,128)(2,1)S(1)} all-gather(bf16[64,1024]{1,0:T(8,128)(2,1)S(1)} %get-tuple-element.917), channel_id=1, replica_groups=mesh['dp'=32,'pipe'=2,'tensor'=4] {'tensor'}, dimensions={1}, use_global_device_ids=true | all-gather | bytes 655360 | tf_op jit(solution)/shard_map/while/body/eval_jaxpr/all_gather | solution.py:92
  768.6 11.5 %conditional.14 = (bf16[64,1024]{1,0:T(8,128)(2,1)S(1)}) conditional(s32[]{:T(128)} %convert_element_type.207, () %tuple.113, (bf16[64,4096]{1,0:T(8,128)(2,1)S(1)}, f32[1,1,4096]{2,1,0:T(1,128)S(1)}, bf16[4096,256]{1,0:T(8,128)(2,1)}, pred[2,64,64]{1,2,0:T(8,128)(4,1)S(1)}, s32[]{:T(128)}, /*index=5*/bf16[4096,256]{1,0:T(8,128)(2,1)}, ...), branch_computations={%region_13.14_spmd, %region_14.18_spmd} | conditional | flops 835764928 | bytes 26319488 | solution.py:104
  768.8 2.1 fusion.81
  771.3 5.2 convolution_bitcast_fusion.1
  780.1 5.0 conditional.15
  780.1 5.0 fusion.102
  785.8 1.6 copy.120
  787.4 3.5 all-to-all-start.1
  794.8 5.9 all-to-all-done.1
  804.0 9.9 %all_gather.32 = bf16[64,4096]{1,0:T(8,128)(2,1)S(1)} all-gather(bf16[64,1024]{1,0:T(8,128)(2,1)S(1)} %bitcast_select_fusion.3), channel_id=1, replica_groups=mesh['dp'=32,'pipe'=2,'tensor'=4] {'tensor'}, dimensions={1}, use_global_device_ids=true | all-gather | bytes 655360 | tf_op jit(solution)/shard_map/while/body/eval_jaxpr/all_gather | solution.py:92
  815.6 11.3 %conditional.12 = (bf16[64,1024]{1,0:T(8,128)(2,1)S(1)}) conditional(s32[]{:T(128)} %convert_element_type.206, () %tuple.109, (bf16[64,4096]{1,0:T(8,128)(2,1)S(1)}, f32[1,1,4096]{2,1,0:T(1,128)S(1)}, bf16[4096,256]{1,0:T(8,128)(2,1)}, s32[]{:T(128)}, pred[2,64,64]{1,2,0:T(8,128)(4,1)S(1)}, /*index=5*/bf16[4096,256]{1,0:T(8,128)(2,1)}, ...), branch_computations={%region_5.6_spmd, %region_6.10_spmd} | conditional | flops 835764928 | bytes 17847848 | solution.py:104
  815.8 2.1 fusion.41
  818.3 5.0 convolution_bitcast_fusion
  824.0 2.1 convolution_convert_fusion.1
  826.9 5.0 conditional.13
  826.9 4.9 fusion.101
  834.1 3.5 all-to-all-start
  837.7 10.6 %all-to-all-done = f32[4,64,1024]{2,1,0:T(8,128)S(1)} async-done(((f32[4,64,1024]{2,1,0:T(8,128)}), f32[4,64,1024]{2,1,0:T(8,128)S(1)}, u32[]{:S(2)}, u32[]{:S(2)}) %all-to-all-start) | async-done | bytes 1048608 | tf_op jit(solution)/shard_map/while/body/eval_jaxpr/all_to_all | solution.py:19
  849.1 9.9 %all_gather.33 = bf16[64,4096]{1,0:T(8,128)(2,1)S(1)} all-gather(bf16[64,1024]{1,0:T(8,128)(2,1)S(1)} %get-tuple-element.917), channel_id=1, replica_groups=mesh['dp'=32,'pipe'=2,'tensor'=4] {'tensor'}, dimensions={1}, use_global_device_ids=true | all-gather | bytes 655360 | tf_op jit(solution)/shard_map/while/body/eval_jaxpr/all_gather | solution.py:92
  859.0 11.5 %conditional.14 = (bf16[64,1024]{1,0:T(8,128)(2,1)S(1)}) conditional(s32[]{:T(128)} %convert_element_type.207, () %tuple.113, (bf16[64,4096]{1,0:T(8,128)(2,1)S(1)}, f32[1,1,4096]{2,1,0:T(1,128)S(1)}, bf16[4096,256]{1,0:T(8,128)(2,1)}, pred[2,64,64]{1,2,0:T(8,128)(4,1)S(1)}, s32[]{:T(128)}, /*index=5*/bf16[4096,256]{1,0:T(8,128)(2,1)}, ...), branch_computations={%region_13.14_spmd, %region_14.18_spmd} | conditional | flops 835764928 | bytes 26319488 | solution.py:104
  859.2 2.1 fusion.81
  861.7 5.2 convolution_bitcast_fusion.1
  870.5 5.0 conditional.15
  870.5 5.0 fusion.102
  877.8 3.5 all-to-all-start.1
  885.1 5.9 all-to-all-done.1
  894.4 9.9 %all_gather.32 = bf16[64,4096]{1,0:T(8,128)(2,1)S(1)} all-gather(bf16[64,1024]{1,0:T(8,128)(2,1)S(1)} %bitcast_select_fusion.3), channel_id=1, replica_groups=mesh['dp'=32,'pipe'=2,'tensor'=4] {'tensor'}, dimensions={1}, use_global_device_ids=true | all-gather | bytes 655360 | tf_op jit(solution)/shard_map/while/body/eval_jaxpr/all_gather | solution.py:92
  908.4 3.5 all-to-all-start
  911.9 11.3 %all-to-all-done = f32[4,64,1024]{2,1,0:T(8,128)S(1)} async-done(((f32[4,64,1024]{2,1,0:T(8,128)}), f32[4,64,1024]{2,1,0:T(8,128)S(1)}, u32[]{:S(2)}, u32[]{:S(2)}) %all-to-all-start) | async-done | bytes 1048608 | tf_op jit(solution)/shard_map/while/body/eval_jaxpr/all_to_all | solution.py:19
  924.0 10.7 %all_gather.33 = bf16[64,4096]{1,0:T(8,128)(2,1)S(1)} all-gather(bf16[64,1024]{1,0:T(8,128)(2,1)S(1)} %get-tuple-element.917), channel_id=1, replica_groups=mesh['dp'=32,'pipe'=2,'tensor'=4] {'tensor'}, dimensions={1}, use_global_device_ids=true | all-gather | bytes 655360 | tf_op jit(solution)/shard_map/while/body/eval_jaxpr/all_gather | solution.py:92
  937.2 3.5 all-to-all-start.1
  944.5 5.9 all-to-all-done.1
  950.5 26.7 %collective-permute-start.1 = (bf16[64,1024]{1,0:T(8,128)(2,1)S(1)}, bf16[64,1024]{1,0:T(8,128)(2,1)S(1)}, u32[]{:S(2)}, u32[]{:S(2)}) collective-permute-start(bf16[64,1024]{1,0:T(8,128)(2,1)S(1)} %get-tuple-element.918), channel_id=1, source_target_pairs={{4,0},{5,1},{6,2},{7,3},{12,8},{13,9},{14,10},{15,11},{20,16},{21,... | collective-permute-start | bytes 393224 | tf_op jit(solution)/shard_map/while/body/eval_jaxpr/ppermute | solution.py:33
  978.2 2.3 all-gather
  (221 shorter events, 62.3 us)
Async XLA Ops:
  6.5 21.7 %copy-start = (bf16[2,64,1024]{2,1,0:T(8,128)(2,1)S(1)}, bf16[2,64,1024]{2,1,0:T(8,128)(2,1)}, u32[]{:S(2)}) copy-start(bf16[2,64,1024]{2,1,0:T(8,128)(2,1)} %param.22) | copy-start | bytes 786436
  6.5 602.8 %all-gather.3.cloned.1.call-start = ((), (), s32[]{:S(2)}) async-start(), calls=%async_computation.3 | async-start | bytes 25952256 | tf_op jit(solution)/shard_map/all_gather | solution.py:26
  15.7 8.6 copy-start.10
  15.7 8.7 copy-start.2
  15.7 11.2 %copy-start.3 = (s32[2]{0:T(128)S(1)}, s32[2]{0:T(128)}, u32[]{:S(2)}) copy-start(s32[2]{0:T(128)} %param.28) | copy-start | bytes 28
  15.7 11.9 %copy-start.4 = (s32[2]{0:T(128)S(1)}, s32[2]{0:T(128)}, u32[]{:S(2)}) copy-start(s32[2]{0:T(128)} %param.29) | copy-start | bytes 28
  15.7 16.6 %copy-start.11 = (f32[2,1,4096]{2,1,0:T(1,128)S(1)}, f32[2,1,4096]{2,1,0:T(1,128)}, u32[]{:S(2)}) copy-start(f32[2,1,4096]{2,1,0:T(1,128)} %param.27) | copy-start | bytes 98308
  15.7 537.1 %all-to-all-start.2 = ((bf16[32,2,1,1024,128]{4,3,2,1,0:T(8,128)(2,1)}), bf16[32,2,1,1024,128]{4,3,2,1,0:T(8,128)(2,1)}, u32[]{:S(2)}, u32[]{:S(2)}) async-start(bf16[32,2,1,1024,128]{4,3,2,1,0:T(8,128)(2,1)} %stack.2), calls=%async_computation.2 | async-start | bytes 33554432 | tf_op jit(solution)/shard_map/all_to_all | solution.py:147
  25.7 1.9 copy-start.12
  643.2 13.2 %all-to-all-start = ((f32[4,64,1024]{2,1,0:T(8,128)}), f32[4,64,1024]{2,1,0:T(8,128)S(1)}, u32[]{:S(2)}, u32[]{:S(2)}) async-start(f32[4,64,1024]{2,1,0:T(8,128)} %copy.119), calls=%async_computation | async-start | bytes 2097152 | tf_op jit(solution)/shard_map/while/body/eval_jaxpr/all_to_all | solution.py:19
  667.1 5.9 copy-start.13
  667.1 8.5 copy-start.6
  669.5 13.3 %all-to-all-start.1 = ((f32[4,64,1024]{2,1,0:T(8,128)}), f32[4,64,1024]{2,1,0:T(8,128)S(1)}, u32[]{:S(2)}, u32[]{:S(2)}) async-start(f32[4,64,1024]{2,1,0:T(8,128)} %copy.120), calls=%async_computation.1 | async-start | bytes 2097152 | tf_op jit(solution)/shard_map/while/body/eval_jaxpr/all_to_all | solution.py:19
  675.6 34.6 %collective-permute-start = (bf16[64,1024]{1,0:T(8,128)(2,1)S(1)}, bf16[64,1024]{1,0:T(8,128)(2,1)}, u32[]{:S(2)}, u32[]{:S(2)}) collective-permute-start(bf16[64,1024]{1,0:T(8,128)(2,1)S(1)} %copy-done.6), channel_id=1, source_target_pairs={{0,4},{1,5},{2,6},{3,7},{8,12},{9,13},{10,14},{11,15},{16,20},{17,... | collective-permute-start | bytes 393224 | tf_op jit(solution)/shard_map/while/body/eval_jaxpr/ppermute | solution.py:33
  682.9 28.2 %collective-permute-start.1 = (bf16[64,1024]{1,0:T(8,128)(2,1)S(1)}, bf16[64,1024]{1,0:T(8,128)(2,1)S(1)}, u32[]{:S(2)}, u32[]{:S(2)}) collective-permute-start(bf16[64,1024]{1,0:T(8,128)(2,1)S(1)} %get-tuple-element.918), channel_id=1, source_target_pairs={{4,0},{5,1},{6,2},{7,3},{12,8},{13,9},{14,10},{15,11},{20,16},{21,... | collective-permute-start | bytes 393224 | tf_op jit(solution)/shard_map/while/body/eval_jaxpr/ppermute | solution.py:33
  742.2 14.9 %all-to-all-start = ((f32[4,64,1024]{2,1,0:T(8,128)}), f32[4,64,1024]{2,1,0:T(8,128)S(1)}, u32[]{:S(2)}, u32[]{:S(2)}) async-start(f32[4,64,1024]{2,1,0:T(8,128)} %copy.119), calls=%async_computation | async-start | bytes 2097152 | tf_op jit(solution)/shard_map/while/body/eval_jaxpr/all_to_all | solution.py:19
  768.8 2.5 copy-start.8
  771.3 5.5 copy-start.7
  771.3 6.1 copy-start.5
  776.8 0.6 copy-start.9
  780.1 10.9 %copy-start.13 = (s32[2]{0:T(128)S(1)}, s32[2]{0:T(128)}, u32[]{:S(2)}) copy-start(s32[2]{0:T(128)} %get-tuple-element.995) | copy-start | bytes 28 | tf_op jit(solution)/shard_map/while
  780.1 13.4 %copy-start.6 = (bf16[64,1024]{1,0:T(8,128)(2,1)S(1)}, bf16[64,1024]{1,0:T(8,128)(2,1)}, u32[]{:S(2)}) copy-start(bf16[64,1024]{1,0:T(8,128)(2,1)} %get-tuple-element.916) | copy-start | bytes 393220 | tf_op jit(solution)/shard_map/while
  787.4 13.2 %all-to-all-start.1 = ((f32[4,64,1024]{2,1,0:T(8,128)}), f32[4,64,1024]{2,1,0:T(8,128)S(1)}, u32[]{:S(2)}, u32[]{:S(2)}) async-start(f32[4,64,1024]{2,1,0:T(8,128)} %copy.120), calls=%async_computation.1 | async-start | bytes 2097152 | tf_op jit(solution)/shard_map/while/body/eval_jaxpr/all_to_all | solution.py:19
  793.5 8.6 collective-permute-start
  800.8 2.3 collective-permute-start.1
  834.1 14.2 %all-to-all-start = ((f32[4,64,1024]{2,1,0:T(8,128)}), f32[4,64,1024]{2,1,0:T(8,128)S(1)}, u32[]{:S(2)}, u32[]{:S(2)}) async-start(f32[4,64,1024]{2,1,0:T(8,128)} %copy.119), calls=%async_computation | async-start | bytes 2097152 | tf_op jit(solution)/shard_map/while/body/eval_jaxpr/all_to_all | solution.py:19
  859.2 2.5 copy-start.8
  861.7 5.5 copy-start.7
  861.7 6.1 copy-start.5
  867.2 0.6 copy-start.9
  870.4 10.9 %copy-start.13 = (s32[2]{0:T(128)S(1)}, s32[2]{0:T(128)}, u32[]{:S(2)}) copy-start(s32[2]{0:T(128)} %get-tuple-element.995) | copy-start | bytes 28 | tf_op jit(solution)/shard_map/while
  870.5 13.4 %copy-start.6 = (bf16[64,1024]{1,0:T(8,128)(2,1)S(1)}, bf16[64,1024]{1,0:T(8,128)(2,1)}, u32[]{:S(2)}) copy-start(bf16[64,1024]{1,0:T(8,128)(2,1)} %get-tuple-element.916) | copy-start | bytes 393220 | tf_op jit(solution)/shard_map/while
  877.8 13.2 %all-to-all-start.1 = ((f32[4,64,1024]{2,1,0:T(8,128)}), f32[4,64,1024]{2,1,0:T(8,128)S(1)}, u32[]{:S(2)}, u32[]{:S(2)}) async-start(f32[4,64,1024]{2,1,0:T(8,128)} %copy.120), calls=%async_computation.1 | async-start | bytes 2097152 | tf_op jit(solution)/shard_map/while/body/eval_jaxpr/all_to_all | solution.py:19
  883.8 8.6 collective-permute-start
  891.1 2.3 collective-permute-start.1
  908.4 14.9 %all-to-all-start = ((f32[4,64,1024]{2,1,0:T(8,128)}), f32[4,64,1024]{2,1,0:T(8,128)S(1)}, u32[]{:S(2)}, u32[]{:S(2)}) async-start(f32[4,64,1024]{2,1,0:T(8,128)} %copy.119), calls=%async_computation | async-start | bytes 2097152 | tf_op jit(solution)/shard_map/while/body/eval_jaxpr/all_to_all | solution.py:19
  934.7 5.9 copy-start.13
  934.7 8.5 copy-start.6
  937.2 13.2 %all-to-all-start.1 = ((f32[4,64,1024]{2,1,0:T(8,128)}), f32[4,64,1024]{2,1,0:T(8,128)S(1)}, u32[]{:S(2)}, u32[]{:S(2)}) async-start(f32[4,64,1024]{2,1,0:T(8,128)} %copy.120), calls=%async_computation.1 | async-start | bytes 2097152 | tf_op jit(solution)/shard_map/while/body/eval_jaxpr/all_to_all | solution.py:19
  943.2 34.0 %collective-permute-start = (bf16[64,1024]{1,0:T(8,128)(2,1)S(1)}, bf16[64,1024]{1,0:T(8,128)(2,1)}, u32[]{:S(2)}, u32[]{:S(2)}) collective-permute-start(bf16[64,1024]{1,0:T(8,128)(2,1)S(1)} %copy-done.6), channel_id=1, source_target_pairs={{0,4},{1,5},{2,6},{3,7},{8,12},{9,13},{10,14},{11,15},{16,20},{17,... | collective-permute-start | bytes 393224 | tf_op jit(solution)/shard_map/while/body/eval_jaxpr/ppermute | solution.py:33
  950.5 27.6 %collective-permute-start.1 = (bf16[64,1024]{1,0:T(8,128)(2,1)S(1)}, bf16[64,1024]{1,0:T(8,128)(2,1)S(1)}, u32[]{:S(2)}, u32[]{:S(2)}) collective-permute-start(bf16[64,1024]{1,0:T(8,128)(2,1)S(1)} %get-tuple-element.918), channel_id=1, source_target_pairs={{4,0},{5,1},{6,2},{7,3},{12,8},{13,9},{14,10},{15,11},{20,16},{21,... | collective-permute-start | bytes 393224 | tf_op jit(solution)/shard_map/while/body/eval_jaxpr/ppermute | solution.py:33
  978.2 3.0 copy-start.1
Sparse Core Ops, SparseCore 0:
  9.9 538.8 all-gather.2
